TPU v7x, 512 devices: a whole 4x4x16 slice. The times are simulated.
512 devices in a mesh: row: 32 (over x, y, core), col: 16 (over z).
Axes of the slice: x: 4, y: 4, z: 16, core: 2. Of those that a mesh axis runs over, the one named last changes fastest.
Arguments:
- features: bfloat16 [65536, 256], P('col', 'row'), may hold values from -6 to 6
- weight: bfloat16 [256, 256], replicated, may hold values from -0.375 to 0.375
- adj_values: bfloat16 [32, 16, 96, 128, 128], P('row', 'col'), may hold values from -0.0625 to 0.0625
- block_rows: int32 [32, 16, 96], P('row', 'col'), may hold values from 0 to 15, as said below
- block_cols: int32 [32, 16, 96], P('row', 'col'), may hold values from 0 to 31
- block_counts: int32 [32, 16], P('row', 'col'), may hold values from 1 to 96, as said below
- cotangent: bfloat16 [65536, 256], P(('row', 'col')), may hold values from -6 to 6
Outputs:
- output: bfloat16 [65536, 256], P(('row', 'col'))
- grad_weight: float32 [256, 256], replicated
- grad_features: bfloat16 [65536, 256], P('col', 'row')
Inputs may be any that keep to these rules, and one draw needn't show every extreme that they name: Within one tile the pairs (block_rows, block_cols) over all 96 slots are distinct. `block_counts`: some tile holds exactly 96 live blocks and some other tile exactly one in every draw.
All inputs are finite; a program needn't handle non-finite values.
Results may differ from a plain program's by a relative error of at most 0.029.
Values may be sent and summed in bfloat16 or wider, within the bound.
A program may use at most 64 MiB of HBM per device.

v0:
```python
import math
import jax
import jax.numpy as jnp
from jax import lax
from jax.sharding import PartitionSpec as P

RB = 16


def block_product(tile_values, tile_rows, tile_cols, live_count, panels, out_blocks, transposed):
    padded = tile_values.shape[0]
    blocks_turn = math.gcd(padded, 16)
    block_size = panels.shape[1]
    columns = panels.shape[2]
    turns_needed = (live_count + blocks_turn - 1) // blocks_turn

    def step(turn_index, running):
        offset = turn_index * blocks_turn
        values_now = lax.dynamic_slice_in_dim(tile_values, offset, blocks_turn, 0)
        row_ids = lax.dynamic_slice_in_dim(tile_rows, offset, blocks_turn, 0)
        col_ids = lax.dynamic_slice_in_dim(tile_cols, offset, blocks_turn, 0)
        is_live = offset + jnp.arange(blocks_turn, dtype=jnp.int32) < live_count
        if transposed:
            picked = jnp.take(panels, row_ids, axis=0)
            product = jnp.einsum(
                "bij,bif->bjf", values_now, picked, preferred_element_type=jnp.float32
            )
            target_ids = col_ids
        else:
            picked = jnp.take(panels, col_ids, axis=0)
            product = jnp.einsum(
                "bij,bjf->bif", values_now, picked, preferred_element_type=jnp.float32
            )
            target_ids = row_ids
        contribution = jnp.where(is_live[:, None, None], product, 0.0)
        return running.at[target_ids].add(contribution)

    start_sum = jnp.zeros((out_blocks, block_size, columns), jnp.float32)
    return lax.fori_loop(0, turns_needed, step, start_sum)


def shards(features, weight, adj_values, block_rows, block_cols, block_counts, cotangent):
    tile_values = adj_values[0, 0]
    tile_rows = block_rows[0, 0]
    tile_cols = block_cols[0, 0]
    live_count = block_counts[0, 0]
    block_size = tile_values.shape[1]
    col_blocks = features.shape[0] // block_size
    node_total = col_blocks * block_size * lax.axis_size("col")
    panel_part = lax.all_gather(features, "row", axis=1, tiled=True)
    panels = panel_part.reshape(col_blocks, block_size, panel_part.shape[1])
    partial_value = block_product(tile_values, tile_rows, tile_cols, live_count, panels, RB, False)
    partial_value = partial_value.reshape(RB * block_size, partial_value.shape[2])
    aggregated = lax.psum_scatter(
        partial_value.astype(jnp.bfloat16), "col", scatter_dimension=0, tiled=True
    )
    preact = jnp.dot(aggregated, weight, preferred_element_type=jnp.float32)
    output = jax.nn.silu(preact).astype(jnp.bfloat16)
    sigmoid_pre = jax.nn.sigmoid(preact)
    slopes = sigmoid_pre * (1.0 + preact * (1.0 - sigmoid_pre))
    deltas = (cotangent.astype(jnp.float32) * slopes).astype(jnp.bfloat16)
    local_grad = jnp.dot(aggregated.T, deltas, preferred_element_type=jnp.float32)
    grad_weight = lax.psum(local_grad, ("row", "col")) * (1.0 / math.sqrt(node_total))
    backward = jnp.dot(deltas, weight.T, preferred_element_type=jnp.float32).astype(jnp.bfloat16)
    back_slab = lax.all_gather(backward, "col", axis=0, tiled=True)
    back_panels = back_slab.reshape(RB, block_size, back_slab.shape[1])
    column_terms = block_product(
        tile_values, tile_rows, tile_cols, live_count, back_panels, col_blocks, True
    )
    column_terms = column_terms.reshape(col_blocks * block_size, column_terms.shape[2])
    grad_features = lax.psum_scatter(
        column_terms.astype(jnp.bfloat16), "row", scatter_dimension=1, tiled=True
    )
    return (output, grad_weight, grad_features)


def solution(mesh):
    return jax.shard_map(
        shards,
        mesh=mesh,
        in_specs=(
            P("col", "row"),
            P(),
            P("row", "col", None, None, None),
            P("row", "col", None),
            P("row", "col", None),
            P("row", "col"),
            P(("row", "col"), None),
        ),
        out_specs=(P(("row", "col"), None), P(), P("col", "row")),
        check_vma=False,
    )
```

profile of v0, /device:TPU:2, one launch (start us, length us, event | category | flops | bytes accessed | tf_op | source)
XLA Modules:
  0.0 847.8 jit_solution(3140927563884392423)
XLA Ops:
  8.6 65.7 %all-gather.3.cloned.1.call-done = bf16[4096,256]{0,1:T(8,128)(2,1)} async-done(((bf16[4096,8]{0,1:T(8,128)(2,1)}), bf16[4096,256]{0,1:T(8,128)(2,1)}) %all-gather.3.cloned.1.call-update) | async-done | bytes 2097168 | tf_op jit(solution)/shard_map/all_gather | solution.py:50
  74.3 4.1 copy.11
  80.0 35.9 %while.20 = (s32[]{:T(128)}, f32[16,128,256]{2,1,0:T(8,128)}, s32[]{:T(128)}, s32[96]{0:T(128)S(1)}, s32[]{:T(128)}, /*index=5*/bf16[96,128,128]{2,1,0:T(8,128)(...) while((s32[]{:T(128)}, f32[16,128,256]{2,1,0:T(8,128)}, ...), condition=%wide.region_2.3_spmd, body=%wide.region_0.2_spmd.sunk | while | flops 135791792 | bytes 12063415 | solution.py:39
  80.7 2.2 gather_fusion
  84.5 4.3 scatter_fusion
  93.4 4.4 scatter_fusion
  98.5 2.2 gather_fusion
  102.4 4.5 scatter_fusion
  107.6 2.2 gather_fusion
  111.4 4.4 scatter_fusion
  115.9 2.8 convert_element_type.24
  118.8 87.5 %reduce-scatter.3.cloned.1.call-done = bf16[128,256]{1,0:T(8,128)(2,1)} async-done(((bf16[2048,256]{1,0:T(8,128)(2,1)}), bf16[128,256]{1,0:T(8,128)(2,1)}) %reduce-scatter.3.cloned.1.call-update) | async-done | bytes 65552 | tf_op jit(solution)/shard_map/reduce_scatter | solution.py:54
  208.9 2.8 copy.10
  212.7 65.3 %all-gather.5.cloned.1.call-done = bf16[2048,256]{1,0:T(8,128)(2,1)} async-done(((bf16[128,256]{1,0:T(8,128)(2,1)}), bf16[2048,256]{1,0:T(8,128)(2,1)}) %all-gather.5.cloned.1.call-update) | async-done | bytes 1048592 | tf_op jit(solution)/shard_map/all_gather | solution.py:65
  278.1 2.4 broadcast_in_dim.59
  280.5 34.6 %while.21 = (s32[]{:T(128)}, f32[32,128,256]{2,1,0:T(8,128)}, s32[]{:T(128)}, s32[96]{0:T(128)S(1)}, s32[]{:T(128)}, /*index=5*/bf16[96,128,128]{1,2,0:T(8,128)(...) while((s32[]{:T(128)}, f32[32,128,256]{2,1,0:T(8,128)}, ...), condition=%wide.region_7.8_spmd, body=%wide.region_5.7_spmd.sunk | while | flops 135791792 | bytes 12063415 | solution.py:39
  284.7 4.3 scatter_fusion.1
  293.3 4.5 scatter_fusion.1
  301.9 4.5 scatter_fusion.1
  310.6 4.4 scatter_fusion.1
  315.1 2.5 convert_element_type.30
  317.6 2.9 copy.15
  320.5 418.5 %all-reduce.2.cloned.1.call-done = f32[256,256]{1,0:T(8,128)} async-done(((f32[256,256]{1,0:T(8,128)}), f32[256,256]{1,0:T(8,128)}) %all-reduce.2.cloned.1.call-update) | async-done | bytes 262160 | tf_op jit(solution)/shard_map/psum | solution.py:63
  740.6 100.6 %reduce-scatter.5.cloned.1.call-done = bf16[4096,8]{0,1:T(8,128)(2,1)} async-done(((bf16[4096,256]{0,1:T(8,128)(2,1)}), bf16[4096,8]{0,1:T(8,128)(2,1)}) %reduce-scatter.5.cloned.1.call-update) | async-done | bytes 65552 | tf_op jit(solution)/shard_map/reduce_scatter | solution.py:71
  (64 shorter events, 36.1 us)
Async XLA Ops:
  7.2 199.1 %copy-start = (bf16[256,256]{1,0:T(8,128)(2,1)S(1)}, bf16[256,256]{1,0:T(8,128)(2,1)}, u32[]{:S(2)}) copy-start(bf16[256,256]{1,0:T(8,128)(2,1)} %param.12) | copy-start | bytes 393220
  7.2 67.2 %all-gather.3.cloned.1.call-start = ((), (), s32[]{:S(2)}) async-start(), calls=%async_computation.2 | async-start | bytes 2162688 | tf_op jit(solution)/shard_map/all_gather | solution.py:50
  7.9 198.4 %reduce-scatter.3.cloned.1.call-start = ((), (), s32[]{:S(2)}) async-start(), calls=%async_computation.3 | async-start | bytes 1114112 | tf_op jit(solution)/shard_map/reduce_scatter | solution.py:54
  78.4 1.5 copy-start.3
  78.4 1.5 copy-start.4
  115.9 90.4 %copy-start.5 = (bf16[128,256]{1,0:T(8,128)(2,1)S(1)}, bf16[128,256]{1,0:T(8,128)(2,1)}, u32[]{:S(2)}) copy-start(bf16[128,256]{1,0:T(8,128)(2,1)} %param.17) | copy-start | bytes 196612
  115.9 93.1 %copy-start.1 = (bf16[96,128,128]{2,1,0:T(8,128)(2,1)S(1)}, bf16[96,128,128]{2,1,0:T(8,128)(2,1)}, u32[]{:S(2)}) copy-start(bf16[96,128,128]{2,1,0:T(8,128)(2,1)} %get-tuple-element.328) | copy-start | bytes 9437188
  118.7 159.3 %all-gather.5.cloned.1.call-start = ((), (), s32[]{:S(2)}) async-start(), calls=%async_computation.5 | async-start | bytes 1114112 | tf_op jit(solution)/shard_map/all_gather | solution.py:65
  208.9 2.9 copy-start.2
  208.9 530.1 %all-reduce.2.cloned.1.call-start = ((), (), s32[]{:S(2)}) async-start(), calls=%async_computation.4 | async-start | bytes 524288 | tf_op jit(solution)/shard_map/psum | solution.py:63
  212.7 628.6 %reduce-scatter.5.cloned.1.call-start = ((), (), s32[]{:S(2)}) async-start(), calls=%async_computation.6 | async-start | bytes 2162688 | tf_op jit(solution)/shard_map/reduce_scatter | solution.py:71
Sparse Core Ops, SparseCore 0:
  11.1 63.1 all-gather.2
  118.9 87.4 reduce-scatter.2
  209.2 68.8 all-gather.4
  284.8 454.1 all-reduce.1
  743.8 97.3 reduce-scatter.4
where the time goes:
time: 850 us; the launch traced here: 848 us
  waiting for transfers between devices  738 us (87%)
  other arithmetic  48.7 us (6%)
  local copies, waits for them, and re-layouts  30 us (4%)
  matrix products  15.8 us (2%)
  between operations  14.5 us (2%)
    psum x1, waiting for transfers between devices, shards(): lax.psum(local_grad, ('row', 'col')) * (1.0 / math.sqrt(node_total))  418 us
    reduce_scatter x1, waiting for transfers between devices, shards(): lax.psum_scatter(column_terms.astype(jnp.bfloat16), 'row', scatter_dimens...  101 us
    reduce_scatter x1, waiting for transfers between devices, shards(): lax.psum_scatter(partial_value.astype(jnp.bfloat16), 'col', scatter_dimen...  87.5 us
    all_gather x1, waiting for transfers between devices, shards(): panel_part = lax.all_gather(features, 'row', axis=1, tiled=True)  65.7 us
    all_gather x1, waiting for transfers between devices, shards(): back_slab = lax.all_gather(backward, 'col', axis=0, tiled=True)  65.3 us
    scatter-add x8, other arithmetic, step(): return running.at[target_ids].add(contribution)  35.2 us
  transfers between devices with their start and end apart: 5, of which 5 were waited for; matrix products, arithmetic and copies ran while one was open for 6% of the time, Pallas kernels for 0%

commit v1 on v0

--- a/solution.py
+++ b/solution.py
@@ -47,7 +47,9 @@
     block_size = tile_values.shape[1]
     col_blocks = features.shape[0] // block_size
     node_total = col_blocks * block_size * lax.axis_size("col")
-    panel_part = lax.all_gather(features, "row", axis=1, tiled=True)
+    panel_part = jnp.concatenate(
+        lax.all_to_all(jnp.stack([features] * lax.axis_size("row")), "row", 0, 0), axis=1
+    )
     panels = panel_part.reshape(col_blocks, block_size, panel_part.shape[1])
     partial_value = block_product(tile_values, tile_rows, tile_cols, live_count, panels, RB, False)
     partial_value = partial_value.reshape(RB * block_size, partial_value.shape[2])

time: 850 us -> 824 us (0.969)
  waiting for transfers between devices: 738 us -> 699 us
  starting transfers between devices: 0.2 us -> 9.78 us
    all_gather x1 -> x0, waiting for transfers between devices: 65.7 us -> none  [shards(): panel_part = lax.all_gather(features, 'row', axis=1, tiled=True)]
    all_to_all x0 -> x1, waiting for transfers between devices: none -> 25.2 us  [shards(): lax.all_to_all(jnp.stack([features] * lax.axis_size('row')), 'row', 0, 0)]
    all_to_all x0 -> x1, starting transfers between devices: none -> 9.62 us  [shards(): lax.all_to_all(jnp.stack([features] * lax.axis_size('row')), 'row', 0, 0)]
where the time goes in v1:
time: 824 us; the launch traced here: 823 us
  waiting for transfers between devices  699 us (85%)
  other arithmetic  48.9 us (6%)
  local copies, waits for them, and re-layouts  34.5 us (4%)
  matrix products  15.8 us (2%)
  between operations  14.5 us (2%)
  starting transfers between devices  9.78 us (1%)
    psum x1, waiting for transfers between devices, shards(): lax.psum(local_grad, ('row', 'col')) * (1.0 / math.sqrt(node_total))  418 us
    reduce_scatter x1, waiting for transfers between devices, shards(): lax.psum_scatter(column_terms.astype(jnp.bfloat16), 'row', scatter_dimens...  101 us
    reduce_scatter x1, waiting for transfers between devices, shards(): lax.psum_scatter(partial_value.astype(jnp.bfloat16), 'col', scatter_dimen...  89.6 us
    all_gather x1, waiting for transfers between devices, shards(): back_slab = lax.all_gather(backward, 'col', axis=0, tiled=True)  65.1 us
    scatter-add x8, other arithmetic, step(): return running.at[target_ids].add(contribution)  35.4 us
    all_to_all x1, waiting for transfers between devices, shards(): lax.all_to_all(jnp.stack([features] * lax.axis_size('row')), 'row', 0, 0)  25.2 us
  transfers between devices with their start and end apart: 5, of which 5 were waited for; matrix products, arithmetic and copies ran while one was open for 6% of the time, Pallas kernels for 0%

profile of v1, /device:TPU:2, one launch (start us, length us, event | category | flops | bytes accessed | tf_op | source)
XLA Modules:
  0.0 822.5 jit_solution(16018705968732496755)
XLA Ops:
  7.2 2.4 stack.2
  9.6 9.6 %all-to-all-start = ((bf16[32,4096,8]{1,2,0:T(8,128)(2,1)}), bf16[32,4096,8]{1,2,0:T(8,128)(2,1)S(1)}, u32[]{:S(2)}, u32[]{:S(2)}) async-start(bf16[32,4096,8]{1,2,0:T(8,128)(2,1)} %stack.2), calls=%async_computation | async-start | bytes 4194304 | tf_op jit(solution)/shard_map/all_to_all | solution.py:51
  20.0 25.2 %all-to-all-done = bf16[32,4096,8]{1,2,0:T(8,128)(2,1)S(1)} async-done(((bf16[32,4096,8]{1,2,0:T(8,128)(2,1)}), bf16[32,4096,8]{1,2,0:T(8,128)(2,1)S(1)}, u32[]{:S(2)}, u32[]{:S(2)}) %all-to-all-start) | async-done | bytes 2097184 | tf_op jit(solution)/shard_map/all_to_all | solution.py:51
  47.0 4.3 copy.16
  52.8 36.0 %while.20 = (s32[]{:T(128)}, f32[16,128,256]{2,1,0:T(8,128)}, s32[]{:T(128)}, s32[96]{0:T(128)S(1)}, s32[]{:T(128)}, /*index=5*/bf16[96,128,128]{2,1,0:T(8,128)(...) while((s32[]{:T(128)}, f32[16,128,256]{2,1,0:T(8,128)}, ...), condition=%wide.region_2.3_spmd, body=%wide.region_0.2_spmd.sunk | while | flops 135791792 | bytes 12063415 | solution.py:39
  53.6 2.2 gather_fusion
  57.4 4.3 scatter_fusion
  66.3 4.4 scatter_fusion
  75.3 4.5 scatter_fusion
  84.3 4.5 scatter_fusion
  88.8 2.8 convert_element_type.24
  91.7 89.6 %reduce-scatter.3.cloned.1.call-done = bf16[128,256]{1,0:T(8,128)(2,1)} async-done(((bf16[2048,256]{1,0:T(8,128)(2,1)}), bf16[128,256]{1,0:T(8,128)(2,1)}) %reduce-scatter.3.cloned.1.call-update) | async-done | bytes 65552 | tf_op jit(solution)/shard_map/reduce_scatter | solution.py:56
  184.0 2.8 copy.14
  187.8 65.1 %all-gather.2.cloned.1.call-done = bf16[2048,256]{1,0:T(8,128)(2,1)} async-done(((bf16[128,256]{1,0:T(8,128)(2,1)}), bf16[2048,256]{1,0:T(8,128)(2,1)}) %all-gather.2.cloned.1.call-update) | async-done | bytes 1048592 | tf_op jit(solution)/shard_map/all_gather | solution.py:67
  252.9 2.4 broadcast_in_dim.59
  255.3 34.6 %while.21 = (s32[]{:T(128)}, f32[32,128,256]{2,1,0:T(8,128)}, s32[]{:T(128)}, s32[96]{0:T(128)S(1)}, s32[]{:T(128)}, /*index=5*/bf16[96,128,128]{1,2,0:T(8,128)(...) while((s32[]{:T(128)}, f32[32,128,256]{2,1,0:T(8,128)}, ...), condition=%wide.region_7.8_spmd, body=%wide.region_5.7_spmd.sunk | while | flops 135791792 | bytes 12063415 | solution.py:39
  259.5 4.3 scatter_fusion.1
  268.1 4.4 scatter_fusion.1
  276.7 4.5 scatter_fusion.1
  285.5 4.5 scatter_fusion.1
  289.9 2.5 convert_element_type.30
  292.4 3.0 copy.19
  295.4 418.3 %all-reduce.2.cloned.1.call-done = f32[256,256]{1,0:T(8,128)} async-done(((f32[256,256]{1,0:T(8,128)}), f32[256,256]{1,0:T(8,128)}) %all-reduce.2.cloned.1.call-update) | async-done | bytes 262160 | tf_op jit(solution)/shard_map/psum | solution.py:65
  715.4 100.6 %reduce-scatter.5.cloned.1.call-done = bf16[4096,8]{0,1:T(8,128)(2,1)} async-done(((bf16[4096,256]{0,1:T(8,128)(2,1)}), bf16[4096,8]{0,1:T(8,128)(2,1)}) %reduce-scatter.5.cloned.1.call-update) | async-done | bytes 65552 | tf_op jit(solution)/shard_map/reduce_scatter | solution.py:73
  (65 shorter events, 41.6 us)
Async XLA Ops:
  7.2 174.2 %copy-start = (bf16[256,256]{1,0:T(8,128)(2,1)S(1)}, bf16[256,256]{1,0:T(8,128)(2,1)}, u32[]{:S(2)}) copy-start(bf16[256,256]{1,0:T(8,128)(2,1)} %param.12) | copy-start | bytes 393220
  9.6 35.6 %all-to-all-start = ((bf16[32,4096,8]{1,2,0:T(8,128)(2,1)}), bf16[32,4096,8]{1,2,0:T(8,128)(2,1)S(1)}, u32[]{:S(2)}, u32[]{:S(2)}) async-start(bf16[32,4096,8]{1,2,0:T(8,128)(2,1)} %stack.2), calls=%async_computation | async-start | bytes 4194304 | tf_op jit(solution)/shard_map/all_to_all | solution.py:51
  19.2 162.1 %reduce-scatter.3.cloned.1.call-start = ((), (), s32[]{:S(2)}) async-start(), calls=%async_computation.3 | async-start | bytes 1114112 | tf_op jit(solution)/shard_map/reduce_scatter | solution.py:56
  51.3 1.5 copy-start.3
  51.3 1.5 copy-start.4
  88.8 92.6 %copy-start.5 = (bf16[128,256]{1,0:T(8,128)(2,1)S(1)}, bf16[128,256]{1,0:T(8,128)(2,1)}, u32[]{:S(2)}) copy-start(bf16[128,256]{1,0:T(8,128)(2,1)} %param.17) | copy-start | bytes 196612
  88.8 95.2 %copy-start.1 = (bf16[96,128,128]{2,1,0:T(8,128)(2,1)S(1)}, bf16[96,128,128]{2,1,0:T(8,128)(2,1)}, u32[]{:S(2)}) copy-start(bf16[96,128,128]{2,1,0:T(8,128)(2,1)} %get-tuple-element.335) | copy-start | bytes 9437188
  91.7 161.2 %all-gather.2.cloned.1.call-start = ((), (), s32[]{:S(2)}) async-start(), calls=%async_computation.5 | async-start | bytes 1114112 | tf_op jit(solution)/shard_map/all_gather | solution.py:67
  183.9 2.9 copy-start.2
  183.9 529.9 %all-reduce.2.cloned.1.call-start = ((), (), s32[]{:S(2)}) async-start(), calls=%async_computation.4 | async-start | bytes 524288 | tf_op jit(solution)/shard_map/psum | solution.py:65
  187.7 628.3 %reduce-scatter.5.cloned.1.call-start = ((), (), s32[]{:S(2)}) async-start(), calls=%async_computation.6 | async-start | bytes 2162688 | tf_op jit(solution)/shard_map/reduce_scatter | solution.py:73
Sparse Core Ops, SparseCore 0:
  91.8 89.5 reduce-scatter.2
  184.2 68.6 all-gather.1
  259.8 453.9 all-reduce.1
  718.6 97.3 reduce-scatter.4
